TPU v7x, 512 devices: a whole 4x4x16 slice. The times are simulated.
512 devices in a mesh: grp: 16 (over z), sub: 32 (over x, y, core).
Axes of the slice: x: 4, y: 4, z: 16, core: 2. Of those that a mesh axis runs over, the one named last changes fastest.
Arguments:
- top_basis: bfloat16 [16, 512, 256], P('grp', 'sub'), may hold values from -0.375 to 0.375
- top_coeffs: bfloat16 [16, 256, 128], P('grp'), may hold values from -6 to 6
- top_coupling: float32 [16, 512, 512], P('grp')
- block_coupling: float32 [16, 32, 128, 512], P('grp', 'sub'), may hold values from -0.09375 to 0.09375
- block_basis: bfloat16 [16, 32, 128, 128], P('grp', 'sub'), may hold values from -0.5 to 0.5
- block_coeffs: bfloat16 [16, 32, 128, 128], P('grp', 'sub'), may hold values from -6 to 6
- sub_basis: bfloat16 [16, 32, 1536, 256], P('grp', 'sub'), may hold values from -0.375 to 0.375
- sub_coeffs: bfloat16 [16, 32, 256, 128], P('grp', 'sub'), may hold values from -6 to 6
- basis_widths: int32 [16, 32], P('grp', 'sub'), may hold values from 32 to 256
- constraint_modes: bfloat16 [16, 32, 1536, 512], P('grp', 'sub'), may hold values from -0.25 to 0.25
- adjacency: int32 [16, 32, 4], P('grp', 'sub'), may hold values from 0 to 4, as said below
Outputs:
- top_values: float32 [16, 512, 128], P('grp')
- block_values: bfloat16 [16, 32, 128, 128], P('grp', 'sub')
- interior: bfloat16 [16, 32, 1536, 128], P('grp', 'sub')
Inputs may be any that keep to these rules, and one draw needn't show every extreme that they name: `adjacency`: the 4 entries of one substructure are different.
All inputs are finite; a program needn't handle non-finite values.
Results may differ from a plain program's by a relative error of at most 0.0044.
Values may be sent and summed in bfloat16 or wider, within the bound.
No kernel may reach another device: no remote copies, remote signals or barrier semaphores. Data moves between devices by JAX's collectives and lax.ppermute only.
A program may use at most 64 MiB of HBM per device.

v0:
```python
import jax
import jax.numpy as jnp
from jax import lax
from jax.sharding import PartitionSpec as P


def from_behind(shard, axis, by):
    peers = lax.axis_size(axis)
    return lax.ppermute(shard, axis, [(i, (i + by) % peers) for i in range(peers)])


def from_behind_2(value, axis, steps):
    count = lax.axis_size(axis)
    first, last = (max(0, -steps), min(count, count - steps))
    return lax.ppermute(value, axis, [(source, source + steps) for source in range(first, last)])


def neighbour_block(block, offset):
    return from_behind(block, "sub", -offset)


def run_chain(top_own, chain_matrix):
    highest = lax.Precision.HIGHEST

    def relay(turn_index, current):
        earlier = from_behind_2(current, "grp", 1)
        return top_own + jnp.dot(chain_matrix, earlier, precision=highest)

    return lax.fori_loop(0, lax.axis_size("grp"), relay, jnp.zeros_like(top_own))


def body(
    top_basis,
    top_coeffs,
    top_coupling,
    block_coupling,
    block_basis,
    block_coeffs,
    sub_basis,
    sub_coeffs,
    basis_widths,
    constraint_modes,
    adjacency,
):
    highest = lax.Precision.HIGHEST
    rows_own = jnp.dot(top_basis[0], top_coeffs[0], preferred_element_type=jnp.float32)
    chain_matrix = top_coupling[0]
    top_own = lax.all_gather(rows_own, "sub", axis=0, tiled=True)
    top_field = run_chain(top_own, chain_matrix)
    own_block = jnp.dot(block_basis[0, 0], block_coeffs[0, 0], preferred_element_type=jnp.float32)
    from_top = jnp.dot(block_coupling[0, 0], top_field, precision=highest)
    block = (own_block + from_top).astype(jnp.bfloat16)
    records = [block, block, block, block, block]
    for offset in (-2, -1, 1, 2):
        records[offset + 2] = neighbour_block(block, offset)
    candidates = jnp.stack(records)
    slots = adjacency[0, 0]
    chosen = jnp.take(candidates, slots, axis=0)
    linked = chosen.reshape(slots.shape[0] * block.shape[0], block.shape[1])
    bound_part = jnp.dot(constraint_modes[0, 0], linked, preferred_element_type=jnp.float32)
    kept_width = basis_widths[0, 0]
    coeffs = sub_coeffs[0, 0]
    basis = sub_basis[0, 0]
    width_total = coeffs.shape[0]
    live_mask = lax.broadcasted_iota(jnp.int32, (width_total, 1), 0) < kept_width
    live_coeffs = jnp.where(live_mask, coeffs, jnp.zeros_like(coeffs))
    fixed_part = jnp.dot(basis, live_coeffs, preferred_element_type=jnp.float32)
    interior = (fixed_part + bound_part).astype(jnp.bfloat16)
    return (top_field[None], block[None, None], interior[None, None])


def solution(mesh):
    placed = (
        P("grp", "sub", None),
        P("grp", None, None),
        P("grp", None, None),
        P("grp", "sub", None, None),
        P("grp", "sub", None, None),
        P("grp", "sub", None, None),
        P("grp", "sub", None, None),
        P("grp", "sub", None, None),
        P("grp", "sub"),
        P("grp", "sub", None, None),
        P("grp", "sub", None),
    )
    return jax.shard_map(
        body,
        mesh=mesh,
        in_specs=placed,
        out_specs=(P("grp", None, None), P("grp", "sub", None, None), P("grp", "sub", None, None)),
        check_vma=False,
    )
```

profile of v0, /device:TPU:384, one launch (start us, length us, event | category | flops | bytes accessed | tf_op | source)
XLA Modules:
  0.0 249.1 jit_solution(1026725116123611253)
XLA Ops:
  1.8 25.2 %all_gather.3 = f32[512,128]{1,0:T(8,128)S(1)} all-gather(f32[16,128]{1,0:T(8,128)S(1)} %fusion.8), channel_id=1, replica_groups=mesh['grp'=16,'sub'=32] {'sub'}, dimensions={0}, use_global_device_ids=true | all-gather | bytes 270336 | tf_op jit(solution)/shard_map/all_gather | solution.py:48
  26.9 199.4 %while.11 = (s32[]{:T(128)}, f32[512,128]{1,0:T(8,128)S(1)}, f32[512,512]{1,0:T(8,128)}, f32[512,128]{1,0:T(8,128)S(1)}, s32[]{:T(128)}, /*index=5*/s32[]{:T(128)}) while((s32[]{:T(128)}, f32[512,128]{1,0:T(8,128)S(1)}, f32[512,512]{1,0:T(8,128)}, f32[512,128]{1,0:T(8,128)S(1)}, s32[]{:T(128)}, /*index=5*/s32[]{:T(128)}) %tuple.30), condition=%wide.region_1.0_spmd.clone, body=%wide.region_0.0_spmd.clone.sunk | while | flops 402784256 | bytes 3407991 | solution.py:29
  27.0 3.1 %collective-permute-start = (f32[512,128]{1,0:T(8,128)S(1)}, f32[512,128]{1,0:T(8,128)S(1)}, u32[]{:S(2)}, u32[]{:S(2)}) collective-permute-start(f32[512,128]{1,0:T(8,128)S(1)} %broadcast_select_fusion.3), channel_id=1, source_target_pairs={{0,32},{32,64},{64,96},{96,128},{128,160},{160,192},{192,224},{224... | collective-permute-start | bytes 786440 | tf_op jit(solution)/shard_map/while/body/eval_jaxpr/ppermute | solution.py:15
  30.0 8.8 %collective-permute-done = f32[512,128]{1,0:T(8,128)S(1)} collective-permute-done((f32[512,128]{1,0:T(8,128)S(1)}, f32[512,128]{1,0:T(8,128)S(1)}, u32[]{:S(2)}, u32[]{:S(2)}) %collective-permute-start) | collective-permute-done | bytes 262176 | tf_op jit(solution)/shard_map/while/body/eval_jaxpr/ppermute | solution.py:15
  38.8 2.2 convolution_add_fusion.4
  43.0 8.9 %collective-permute-done = f32[512,128]{1,0:T(8,128)S(1)} collective-permute-done((f32[512,128]{1,0:T(8,128)S(1)}, f32[512,128]{1,0:T(8,128)S(1)}, u32[]{:S(2)}, u32[]{:S(2)}) %collective-permute-start) | collective-permute-done | bytes 262176 | tf_op jit(solution)/shard_map/while/body/eval_jaxpr/ppermute | solution.py:15
  51.9 2.2 convolution_add_fusion.4
  56.1 8.0 %collective-permute-done = f32[512,128]{1,0:T(8,128)S(1)} collective-permute-done((f32[512,128]{1,0:T(8,128)S(1)}, f32[512,128]{1,0:T(8,128)S(1)}, u32[]{:S(2)}, u32[]{:S(2)}) %collective-permute-start) | collective-permute-done | bytes 262176 | tf_op jit(solution)/shard_map/while/body/eval_jaxpr/ppermute | solution.py:15
  64.1 2.2 convolution_add_fusion.4
  68.3 7.5 %collective-permute-done = f32[512,128]{1,0:T(8,128)S(1)} collective-permute-done((f32[512,128]{1,0:T(8,128)S(1)}, f32[512,128]{1,0:T(8,128)S(1)}, u32[]{:S(2)}, u32[]{:S(2)}) %collective-permute-start) | collective-permute-done | bytes 262176 | tf_op jit(solution)/shard_map/while/body/eval_jaxpr/ppermute | solution.py:15
  75.9 2.2 convolution_add_fusion.4
  80.0 7.5 %collective-permute-done = f32[512,128]{1,0:T(8,128)S(1)} collective-permute-done((f32[512,128]{1,0:T(8,128)S(1)}, f32[512,128]{1,0:T(8,128)S(1)}, u32[]{:S(2)}, u32[]{:S(2)}) %collective-permute-start) | collective-permute-done | bytes 262176 | tf_op jit(solution)/shard_map/while/body/eval_jaxpr/ppermute | solution.py:15
  87.6 2.2 convolution_add_fusion.4
  91.8 7.5 %collective-permute-done = f32[512,128]{1,0:T(8,128)S(1)} collective-permute-done((f32[512,128]{1,0:T(8,128)S(1)}, f32[512,128]{1,0:T(8,128)S(1)}, u32[]{:S(2)}, u32[]{:S(2)}) %collective-permute-start) | collective-permute-done | bytes 262176 | tf_op jit(solution)/shard_map/while/body/eval_jaxpr/ppermute | solution.py:15
  99.3 2.2 convolution_add_fusion.4
  103.5 7.5 %collective-permute-done = f32[512,128]{1,0:T(8,128)S(1)} collective-permute-done((f32[512,128]{1,0:T(8,128)S(1)}, f32[512,128]{1,0:T(8,128)S(1)}, u32[]{:S(2)}, u32[]{:S(2)}) %collective-permute-start) | collective-permute-done | bytes 262176 | tf_op jit(solution)/shard_map/while/body/eval_jaxpr/ppermute | solution.py:15
  111.1 2.2 convolution_add_fusion.4
  115.3 7.6 %collective-permute-done = f32[512,128]{1,0:T(8,128)S(1)} collective-permute-done((f32[512,128]{1,0:T(8,128)S(1)}, f32[512,128]{1,0:T(8,128)S(1)}, u32[]{:S(2)}, u32[]{:S(2)}) %collective-permute-start) | collective-permute-done | bytes 262176 | tf_op jit(solution)/shard_map/while/body/eval_jaxpr/ppermute | solution.py:15
  127.0 8.7 %collective-permute-done = f32[512,128]{1,0:T(8,128)S(1)} collective-permute-done((f32[512,128]{1,0:T(8,128)S(1)}, f32[512,128]{1,0:T(8,128)S(1)}, u32[]{:S(2)}, u32[]{:S(2)}) %collective-permute-start) | collective-permute-done | bytes 262176 | tf_op jit(solution)/shard_map/while/body/eval_jaxpr/ppermute | solution.py:15
  139.9 9.9 %collective-permute-done = f32[512,128]{1,0:T(8,128)S(1)} collective-permute-done((f32[512,128]{1,0:T(8,128)S(1)}, f32[512,128]{1,0:T(8,128)S(1)}, u32[]{:S(2)}, u32[]{:S(2)}) %collective-permute-start) | collective-permute-done | bytes 262176 | tf_op jit(solution)/shard_map/while/body/eval_jaxpr/ppermute | solution.py:15
  153.9 9.7 %collective-permute-done = f32[512,128]{1,0:T(8,128)S(1)} collective-permute-done((f32[512,128]{1,0:T(8,128)S(1)}, f32[512,128]{1,0:T(8,128)S(1)}, u32[]{:S(2)}, u32[]{:S(2)}) %collective-permute-start) | collective-permute-done | bytes 262176 | tf_op jit(solution)/shard_map/while/body/eval_jaxpr/ppermute | solution.py:15
  163.6 2.2 convolution_add_fusion.4
  167.8 8.9 %collective-permute-done = f32[512,128]{1,0:T(8,128)S(1)} collective-permute-done((f32[512,128]{1,0:T(8,128)S(1)}, f32[512,128]{1,0:T(8,128)S(1)}, u32[]{:S(2)}, u32[]{:S(2)}) %collective-permute-start) | collective-permute-done | bytes 262176 | tf_op jit(solution)/shard_map/while/body/eval_jaxpr/ppermute | solution.py:15
  176.7 2.2 convolution_add_fusion.4
  180.9 8.0 %collective-permute-done = f32[512,128]{1,0:T(8,128)S(1)} collective-permute-done((f32[512,128]{1,0:T(8,128)S(1)}, f32[512,128]{1,0:T(8,128)S(1)}, u32[]{:S(2)}, u32[]{:S(2)}) %collective-permute-start) | collective-permute-done | bytes 262176 | tf_op jit(solution)/shard_map/while/body/eval_jaxpr/ppermute | solution.py:15
  188.9 2.2 convolution_add_fusion.4
  193.1 7.5 %collective-permute-done = f32[512,128]{1,0:T(8,128)S(1)} collective-permute-done((f32[512,128]{1,0:T(8,128)S(1)}, f32[512,128]{1,0:T(8,128)S(1)}, u32[]{:S(2)}, u32[]{:S(2)}) %collective-permute-start) | collective-permute-done | bytes 262176 | tf_op jit(solution)/shard_map/while/body/eval_jaxpr/ppermute | solution.py:15
  204.8 7.5 %collective-permute-done = f32[512,128]{1,0:T(8,128)S(1)} collective-permute-done((f32[512,128]{1,0:T(8,128)S(1)}, f32[512,128]{1,0:T(8,128)S(1)}, u32[]{:S(2)}, u32[]{:S(2)}) %collective-permute-start) | collective-permute-done | bytes 262176 | tf_op jit(solution)/shard_map/while/body/eval_jaxpr/ppermute | solution.py:15
  216.5 7.5 %collective-permute-done = f32[512,128]{1,0:T(8,128)S(1)} collective-permute-done((f32[512,128]{1,0:T(8,128)S(1)}, f32[512,128]{1,0:T(8,128)S(1)}, u32[]{:S(2)}, u32[]{:S(2)}) %collective-permute-start) | collective-permute-done | bytes 262176 | tf_op jit(solution)/shard_map/while/body/eval_jaxpr/ppermute | solution.py:15
  228.7 4.6 %collective-permute-start.4 = (bf16[128,128]{1,0:T(8,128)(2,1)S(1)}, bf16[128,128]{1,0:T(8,128)(2,1)S(1)}, u32[]{:S(2)}, u32[]{:S(2)}) collective-permute-start(bf16[128,128]{1,0:T(8,128)(2,1)S(1)} %fusion.3), channel_id=1, source_target_pairs={{0,30},{1,31},{2,0},{3,1},{4,2},{5,3},{6,4},{7,5},{8,6},{9,7},{10,... | collective-permute-start | bytes 98312 | tf_op jit(solution)/shard_map/ppermute | solution.py:9
  235.2 2.4 collective-permute-start.2
  240.8 6.0 %collective-permute-done.1 = bf16[128,128]{1,0:T(8,128)(2,1)S(1)} collective-permute-done((bf16[128,128]{1,0:T(8,128)(2,1)S(1)}, bf16[128,128]{1,0:T(8,128)(2,1)S(1)}, u32[]{:S(2)}, u32[]{:S(2)}) %collective-permute-start.1) | collective-permute-done | bytes 32800 | tf_op jit(solution)/shard_map/ppermute | solution.py:9
  (74 shorter events, 52.5 us)
Async XLA Ops:
  0.6 246.9 %copy-start = (bf16[1,1,1536,512]{3,2,1,0:T(8,128)(2,1)S(1)}, bf16[1,1,1536,512]{3,2,1,0:T(8,128)(2,1)}, u32[]{:S(2)}) copy-start(bf16[1,1,1536,512]{3,2,1,0:T(8,128)(2,1)} %param.22) | copy-start | bytes 4718596
  26.9 200.9 %copy-start.5 = (bf16[1,1,128,128]{3,2,1,0:T(8,128)(2,1)S(1)}, bf16[1,1,128,128]{3,2,1,0:T(8,128)(2,1)}, u32[]{:S(2)}) copy-start(bf16[1,1,128,128]{3,2,1,0:T(8,128)(2,1)} %param.18) | copy-start | bytes 98308
  26.9 212.7 %copy-start.6 = (s32[1,1,4]{2,1,0:T(1,128)S(1)}, s32[1,1,4]{2,1,0:T(1,128)}, u32[]{:S(2)}) copy-start(s32[1,1,4]{2,1,0:T(1,128)} %param.23) | copy-start | bytes 52
  26.9 213.4 %copy-start.2 = (bf16[1,1,1536,256]{3,2,1,0:T(8,128)(2,1)S(1)}, bf16[1,1,1536,256]{3,2,1,0:T(8,128)(2,1)}, u32[]{:S(2)}) copy-start(bf16[1,1,1536,256]{3,2,1,0:T(8,128)(2,1)} %param.19) | copy-start | bytes 2359300
  26.9 213.4 %copy-start.4 = (bf16[1,1,256,128]{3,2,1,0:T(8,128)(2,1)S(1)}, bf16[1,1,256,128]{3,2,1,0:T(8,128)(2,1)}, u32[]{:S(2)}) copy-start(bf16[1,1,256,128]{3,2,1,0:T(8,128)(2,1)} %param.20) | copy-start | bytes 196612
  27.0 11.8 %collective-permute-start = (f32[512,128]{1,0:T(8,128)S(1)}, f32[512,128]{1,0:T(8,128)S(1)}, u32[]{:S(2)}, u32[]{:S(2)}) collective-permute-start(f32[512,128]{1,0:T(8,128)S(1)} %broadcast_select_fusion.3), channel_id=1, source_target_pairs={{0,32},{32,64},{64,96},{96,128},{128,160},{160,192},{192,224},{224... | collective-permute-start | bytes 786440 | tf_op jit(solution)/shard_map/while/body/eval_jaxpr/ppermute | solution.py:15
  41.0 10.8 %collective-permute-start = (f32[512,128]{1,0:T(8,128)S(1)}, f32[512,128]{1,0:T(8,128)S(1)}, u32[]{:S(2)}, u32[]{:S(2)}) collective-permute-start(f32[512,128]{1,0:T(8,128)S(1)} %broadcast_select_fusion.3), channel_id=1, source_target_pairs={{0,32},{32,64},{64,96},{96,128},{128,160},{160,192},{192,224},{224... | collective-permute-start | bytes 786440 | tf_op jit(solution)/shard_map/while/body/eval_jaxpr/ppermute | solution.py:15
  54.1 10.0 %collective-permute-start = (f32[512,128]{1,0:T(8,128)S(1)}, f32[512,128]{1,0:T(8,128)S(1)}, u32[]{:S(2)}, u32[]{:S(2)}) collective-permute-start(f32[512,128]{1,0:T(8,128)S(1)} %broadcast_select_fusion.3), channel_id=1, source_target_pairs={{0,32},{32,64},{64,96},{96,128},{128,160},{160,192},{192,224},{224... | collective-permute-start | bytes 786440 | tf_op jit(solution)/shard_map/while/body/eval_jaxpr/ppermute | solution.py:15
  66.4 9.5 %collective-permute-start = (f32[512,128]{1,0:T(8,128)S(1)}, f32[512,128]{1,0:T(8,128)S(1)}, u32[]{:S(2)}, u32[]{:S(2)}) collective-permute-start(f32[512,128]{1,0:T(8,128)S(1)} %broadcast_select_fusion.3), channel_id=1, source_target_pairs={{0,32},{32,64},{64,96},{96,128},{128,160},{160,192},{192,224},{224... | collective-permute-start | bytes 786440 | tf_op jit(solution)/shard_map/while/body/eval_jaxpr/ppermute | solution.py:15
  78.1 9.5 %collective-permute-start = (f32[512,128]{1,0:T(8,128)S(1)}, f32[512,128]{1,0:T(8,128)S(1)}, u32[]{:S(2)}, u32[]{:S(2)}) collective-permute-start(f32[512,128]{1,0:T(8,128)S(1)} %broadcast_select_fusion.3), channel_id=1, source_target_pairs={{0,32},{32,64},{64,96},{96,128},{128,160},{160,192},{192,224},{224... | collective-permute-start | bytes 786440 | tf_op jit(solution)/shard_map/while/body/eval_jaxpr/ppermute | solution.py:15
  89.9 9.5 %collective-permute-start = (f32[512,128]{1,0:T(8,128)S(1)}, f32[512,128]{1,0:T(8,128)S(1)}, u32[]{:S(2)}, u32[]{:S(2)}) collective-permute-start(f32[512,128]{1,0:T(8,128)S(1)} %broadcast_select_fusion.3), channel_id=1, source_target_pairs={{0,32},{32,64},{64,96},{96,128},{128,160},{160,192},{192,224},{224... | collective-permute-start | bytes 786440 | tf_op jit(solution)/shard_map/while/body/eval_jaxpr/ppermute | solution.py:15
  101.6 9.5 %collective-permute-start = (f32[512,128]{1,0:T(8,128)S(1)}, f32[512,128]{1,0:T(8,128)S(1)}, u32[]{:S(2)}, u32[]{:S(2)}) collective-permute-start(f32[512,128]{1,0:T(8,128)S(1)} %broadcast_select_fusion.3), channel_id=1, source_target_pairs={{0,32},{32,64},{64,96},{96,128},{128,160},{160,192},{192,224},{224... | collective-permute-start | bytes 786440 | tf_op jit(solution)/shard_map/while/body/eval_jaxpr/ppermute | solution.py:15
  113.3 9.5 %collective-permute-start = (f32[512,128]{1,0:T(8,128)S(1)}, f32[512,128]{1,0:T(8,128)S(1)}, u32[]{:S(2)}, u32[]{:S(2)}) collective-permute-start(f32[512,128]{1,0:T(8,128)S(1)} %broadcast_select_fusion.3), channel_id=1, source_target_pairs={{0,32},{32,64},{64,96},{96,128},{128,160},{160,192},{192,224},{224... | collective-permute-start | bytes 786440 | tf_op jit(solution)/shard_map/while/body/eval_jaxpr/ppermute | solution.py:15
  125.1 10.6 %collective-permute-start = (f32[512,128]{1,0:T(8,128)S(1)}, f32[512,128]{1,0:T(8,128)S(1)}, u32[]{:S(2)}, u32[]{:S(2)}) collective-permute-start(f32[512,128]{1,0:T(8,128)S(1)} %broadcast_select_fusion.3), channel_id=1, source_target_pairs={{0,32},{32,64},{64,96},{96,128},{128,160},{160,192},{192,224},{224... | collective-permute-start | bytes 786440 | tf_op jit(solution)/shard_map/while/body/eval_jaxpr/ppermute | solution.py:15
  138.0 11.8 %collective-permute-start = (f32[512,128]{1,0:T(8,128)S(1)}, f32[512,128]{1,0:T(8,128)S(1)}, u32[]{:S(2)}, u32[]{:S(2)}) collective-permute-start(f32[512,128]{1,0:T(8,128)S(1)} %broadcast_select_fusion.3), channel_id=1, source_target_pairs={{0,32},{32,64},{64,96},{96,128},{128,160},{160,192},{192,224},{224... | collective-permute-start | bytes 786440 | tf_op jit(solution)/shard_map/while/body/eval_jaxpr/ppermute | solution.py:15
  152.0 11.6 %collective-permute-start = (f32[512,128]{1,0:T(8,128)S(1)}, f32[512,128]{1,0:T(8,128)S(1)}, u32[]{:S(2)}, u32[]{:S(2)}) collective-permute-start(f32[512,128]{1,0:T(8,128)S(1)} %broadcast_select_fusion.3), channel_id=1, source_target_pairs={{0,32},{32,64},{64,96},{96,128},{128,160},{160,192},{192,224},{224... | collective-permute-start | bytes 786440 | tf_op jit(solution)/shard_map/while/body/eval_jaxpr/ppermute | solution.py:15
  165.9 10.8 %collective-permute-start = (f32[512,128]{1,0:T(8,128)S(1)}, f32[512,128]{1,0:T(8,128)S(1)}, u32[]{:S(2)}, u32[]{:S(2)}) collective-permute-start(f32[512,128]{1,0:T(8,128)S(1)} %broadcast_select_fusion.3), channel_id=1, source_target_pairs={{0,32},{32,64},{64,96},{96,128},{128,160},{160,192},{192,224},{224... | collective-permute-start | bytes 786440 | tf_op jit(solution)/shard_map/while/body/eval_jaxpr/ppermute | solution.py:15
  179.0 9.9 %collective-permute-start = (f32[512,128]{1,0:T(8,128)S(1)}, f32[512,128]{1,0:T(8,128)S(1)}, u32[]{:S(2)}, u32[]{:S(2)}) collective-permute-start(f32[512,128]{1,0:T(8,128)S(1)} %broadcast_select_fusion.3), channel_id=1, source_target_pairs={{0,32},{32,64},{64,96},{96,128},{128,160},{160,192},{192,224},{224... | collective-permute-start | bytes 786440 | tf_op jit(solution)/shard_map/while/body/eval_jaxpr/ppermute | solution.py:15
  191.1 9.5 %collective-permute-start = (f32[512,128]{1,0:T(8,128)S(1)}, f32[512,128]{1,0:T(8,128)S(1)}, u32[]{:S(2)}, u32[]{:S(2)}) collective-permute-start(f32[512,128]{1,0:T(8,128)S(1)} %broadcast_select_fusion.3), channel_id=1, source_target_pairs={{0,32},{32,64},{64,96},{96,128},{128,160},{160,192},{192,224},{224... | collective-permute-start | bytes 786440 | tf_op jit(solution)/shard_map/while/body/eval_jaxpr/ppermute | solution.py:15
  202.9 9.5 %collective-permute-start = (f32[512,128]{1,0:T(8,128)S(1)}, f32[512,128]{1,0:T(8,128)S(1)}, u32[]{:S(2)}, u32[]{:S(2)}) collective-permute-start(f32[512,128]{1,0:T(8,128)S(1)} %broadcast_select_fusion.3), channel_id=1, source_target_pairs={{0,32},{32,64},{64,96},{96,128},{128,160},{160,192},{192,224},{224... | collective-permute-start | bytes 786440 | tf_op jit(solution)/shard_map/while/body/eval_jaxpr/ppermute | solution.py:15
  214.6 9.5 %collective-permute-start = (f32[512,128]{1,0:T(8,128)S(1)}, f32[512,128]{1,0:T(8,128)S(1)}, u32[]{:S(2)}, u32[]{:S(2)}) collective-permute-start(f32[512,128]{1,0:T(8,128)S(1)} %broadcast_select_fusion.3), channel_id=1, source_target_pairs={{0,32},{32,64},{64,96},{96,128},{128,160},{160,192},{192,224},{224... | collective-permute-start | bytes 786440 | tf_op jit(solution)/shard_map/while/body/eval_jaxpr/ppermute | solution.py:15
  226.3 21.2 %copy-start.1 = (f32[512,128]{1,0:T(8,128)}, f32[512,128]{1,0:T(8,128)S(1)}, u32[]{:S(2)}) copy-start(f32[512,128]{1,0:T(8,128)S(1)} %get-tuple-element.25) | copy-start | bytes 786436
  228.7 19.5 %copy-start.3 = (bf16[128,128]{1,0:T(8,128)(2,1)}, bf16[128,128]{1,0:T(8,128)(2,1)S(1)}, u32[]{:S(2)}) copy-start(bf16[128,128]{1,0:T(8,128)(2,1)S(1)} %fusion.3) | copy-start | bytes 98308
  228.7 18.1 %collective-permute-start.4 = (bf16[128,128]{1,0:T(8,128)(2,1)S(1)}, bf16[128,128]{1,0:T(8,128)(2,1)S(1)}, u32[]{:S(2)}, u32[]{:S(2)}) collective-permute-start(bf16[128,128]{1,0:T(8,128)(2,1)S(1)} %fusion.3), channel_id=1, source_target_pairs={{0,30},{1,31},{2,0},{3,1},{4,2},{5,3},{6,4},{7,5},{8,6},{9,7},{10,... | collective-permute-start | bytes 98312 | tf_op jit(solution)/shard_map/ppermute | solution.py:9
  233.3 13.5 %collective-permute-start.3 = (bf16[128,128]{1,0:T(8,128)(2,1)S(1)}, bf16[128,128]{1,0:T(8,128)(2,1)S(1)}, u32[]{:S(2)}, u32[]{:S(2)}) collective-permute-start(bf16[128,128]{1,0:T(8,128)(2,1)S(1)} %fusion.3), channel_id=1, source_target_pairs={{0,31},{1,0},{2,1},{3,2},{4,3},{5,4},{6,5},{7,6},{8,7},{9,8},{10,9... | collective-permute-start | bytes 98312 | tf_op jit(solution)/shard_map/ppermute | solution.py:9
  235.2 11.5 %collective-permute-start.2 = (bf16[128,128]{1,0:T(8,128)(2,1)S(1)}, bf16[128,128]{1,0:T(8,128)(2,1)S(1)}, u32[]{:S(2)}, u32[]{:S(2)}) collective-permute-start(bf16[128,128]{1,0:T(8,128)(2,1)S(1)} %fusion.3), channel_id=1, source_target_pairs={{0,1},{1,2},{2,3},{3,4},{4,5},{5,6},{6,7},{7,8},{8,9},{9,10},{10,1... | collective-permute-start | bytes 98312 | tf_op jit(solution)/shard_map/ppermute | solution.py:9
  237.7 9.1 %collective-permute-start.1 = (bf16[128,128]{1,0:T(8,128)(2,1)S(1)}, bf16[128,128]{1,0:T(8,128)(2,1)S(1)}, u32[]{:S(2)}, u32[]{:S(2)}) collective-permute-start(bf16[128,128]{1,0:T(8,128)(2,1)S(1)} %fusion.3), channel_id=1, source_target_pairs={{0,2},{1,3},{2,4},{3,5},{4,6},{5,7},{6,8},{7,9},{8,10},{9,11},{10,... | collective-permute-start | bytes 98312 | tf_op jit(solution)/shard_map/ppermute | solution.py:9
where the time goes:
time: 251 us; the launch traced here: 249 us
  waiting for transfers between devices  137 us (55%)
  starting transfers between devices  42.7 us (17%)
  matrix products  39.9 us (16%)
  blocking collectives  25.2 us (10%)
    ppermute x16, waiting for transfers between devices, from_behind_2(): lax.ppermute(value, axis, [(source, source + steps) for source in range(f...  131 us
    dot_general x16, matrix products, relay(): return top_own + jnp.dot(chain_matrix, earlier, precision=highest)  35.4 us
    ppermute x16, starting transfers between devices, from_behind_2(): lax.ppermute(value, axis, [(source, source + steps) for source in range(f...  31.9 us
    all_gather x1, blocking collectives, body(): top_own = lax.all_gather(rows_own, 'sub', axis=0, tiled=True)  25.2 us
    ppermute x4, starting transfers between devices, from_behind(): lax.ppermute(shard, axis, [(i, (i + by) % peers) for i in range(peers)])  10.8 us
    ppermute x4, waiting for transfers between devices, from_behind(): lax.ppermute(shard, axis, [(i, (i + by) % peers) for i in range(peers)])  6 us
  transfers between devices with their start and end apart: 20, of which 17 were waited for; matrix products, arithmetic and copies ran while one was open for 0% of the time, Pallas kernels for 0%

commit v1 on v0

--- a/solution.py
+++ b/solution.py
@@ -2,6 +2,7 @@
 import jax.numpy as jnp
 from jax import lax
 from jax.sharding import PartitionSpec as P
+from jax.lax import all_to_all, axis_size
 
 
 def from_behind(shard, axis, by):
@@ -45,7 +46,15 @@
     highest = lax.Precision.HIGHEST
     rows_own = jnp.dot(top_basis[0], top_coeffs[0], preferred_element_type=jnp.float32)
     chain_matrix = top_coupling[0]
-    top_own = lax.all_gather(rows_own, "sub", axis=0, tiled=True)
+    top_own = jnp.concatenate(
+        all_to_all(
+            jnp.stack([rows_own for _ in range(axis_size("sub"))], axis=0),
+            "sub",
+            split_axis=0,
+            concat_axis=0,
+        ),
+        axis=0,
+    )
     top_field = run_chain(top_own, chain_matrix)
     own_block = jnp.dot(block_basis[0, 0], block_coeffs[0, 0], preferred_element_type=jnp.float32)
     from_top = jnp.dot(block_coupling[0, 0], top_field, precision=highest)

time: 251 us -> 237 us (0.944)
  the two profiles are of different devices: /device:TPU:384 before, /device:TPU:256 now
where the time goes in v1:
time: 237 us
  waiting for transfers between devices  145 us (61%)
  starting transfers between devices  52.3 us (22%)
  matrix products  21.7 us (9%)
  other arithmetic  13 us (5%)
    ppermute x16, waiting for transfers between devices, from_behind_2(): lax.ppermute(value, axis, [(source, source + steps) for source in range(f...  135 us
    ppermute x16, starting transfers between devices, from_behind_2(): lax.ppermute(value, axis, [(source, source + steps) for source in range(f...  31.5 us
    dot_general x16, matrix products, relay(): return top_own + jnp.dot(chain_matrix, earlier, precision=highest)  15.8 us
    ppermute x4, starting transfers between devices, from_behind(): lax.ppermute(shard, axis, [(i, (i + by) % peers) for i in range(peers)])  13.5 us
    while x16, other arithmetic  11.6 us
    all_to_all x1, starting transfers between devices, body(): all_to_all(jnp.stack([rows_own for _ in range(axis_size('sub'))], axis=0)...  7.32 us
    ppermute x4, waiting for transfers between devices, from_behind(): lax.ppermute(shard, axis, [(i, (i + by) % peers) for i in range(peers)])  6.12 us
  transfers between devices with their start and end apart: 21, of which 18 were waited for; matrix products, arithmetic and copies ran while one was open for 2% of the time, Pallas kernels for 0%

profile of v1, /device:TPU:256, one launch (start us, length us, event | category | flops | bytes accessed | tf_op | source)
XLA Modules:
  0.0 236.7 jit_solution(6276279531791011911)
XLA Ops:
  2.5 7.3 %all-to-all-start = ((f32[32,16,128]{2,1,0:T(8,128)}), f32[32,16,128]{2,1,0:T(8,128)S(1)}, u32[]{:S(2)}, u32[]{:S(2)}) async-start(f32[32,16,128]{2,1,0:T(8,128)} %stack.14), calls=%async_computation | async-start | bytes 524288 | tf_op jit(solution)/shard_map/all_to_all | solution.py:50
  11.8 2.6 %fusion.4 = f32[128,1536]{1,0:T(8,128)} fusion(bf16[1,1,1536,256]{3,2,1,0:T(8,128)(2,1)} %param.19, bf16[1,1,256,128]{3,2,1,0:T(8,128)(2,1)} %param.20, pred[256]{0:T(512)(128)(4,1)S(1)} %iota_compare_fusion), kind=kOutput, calls=%fused_computation.10 | convolution fusion | flops 100696064 | bytes 1638656 | tf_op jit(solution)/shard_map/dot_general | solution.py:76
  14.4 4.4 %all-to-all-done = f32[32,16,128]{2,1,0:T(8,128)S(1)} async-done(((f32[32,16,128]{2,1,0:T(8,128)}), f32[32,16,128]{2,1,0:T(8,128)S(1)}, u32[]{:S(2)}, u32[]{:S(2)}) %all-to-all-start) | async-done | bytes 262176 | tf_op jit(solution)/shard_map/all_to_all | solution.py:50
  18.8 194.2 %while.11 = (s32[]{:T(128)}, f32[512,128]{1,0:T(8,128)S(1)}, f32[512,512]{1,0:T(8,128)S(1)}, f32[512,128]{1,0:T(8,128)S(1)}, s32[]{:T(128)}, /*index=5*/s32[]{:T(128)}) while((s32[]{:T(128)}, f32[512,128]{1,0:T(8,128)S(1)}, f32[512,512]{1,0:T(8,128)S(1)}, f32[512,128]{1,0:T(8,128)S(1)}, s32[]{:T(128)}, /*index=5*/s32[]{:T(128)}) %tuple.31), condition=%wide.region_1.0_spmd.clone, body=%wide.region_0.0_spmd.clone.sunk | while | flops 402784256 | bytes 3407991 | solution.py:30
  19.5 2.9 %collective-permute-start = (f32[512,128]{1,0:T(8,128)}, f32[512,128]{1,0:T(8,128)S(1)}, u32[]{:S(2)}, u32[]{:S(2)}) collective-permute-start(f32[512,128]{1,0:T(8,128)} %broadcast_select_fusion.3), channel_id=1, source_target_pairs={{0,32},{32,64},{64,96},{96,128},{128,160},{160,192},{192,224},{224... | collective-permute-start | bytes 786440 | tf_op jit(solution)/shard_map/while/body/eval_jaxpr/ppermute | solution.py:16
  22.4 8.9 %collective-permute-done = f32[512,128]{1,0:T(8,128)S(1)} collective-permute-done((f32[512,128]{1,0:T(8,128)}, f32[512,128]{1,0:T(8,128)S(1)}, u32[]{:S(2)}, u32[]{:S(2)}) %collective-permute-start) | collective-permute-done | bytes 262176 | tf_op jit(solution)/shard_map/while/body/eval_jaxpr/ppermute | solution.py:16
  35.0 9.1 %collective-permute-done = f32[512,128]{1,0:T(8,128)S(1)} collective-permute-done((f32[512,128]{1,0:T(8,128)}, f32[512,128]{1,0:T(8,128)S(1)}, u32[]{:S(2)}, u32[]{:S(2)}) %collective-permute-start) | collective-permute-done | bytes 262176 | tf_op jit(solution)/shard_map/while/body/eval_jaxpr/ppermute | solution.py:16
  45.8 1.9 collective-permute-start
  47.7 8.2 %collective-permute-done = f32[512,128]{1,0:T(8,128)S(1)} collective-permute-done((f32[512,128]{1,0:T(8,128)}, f32[512,128]{1,0:T(8,128)S(1)}, u32[]{:S(2)}, u32[]{:S(2)}) %collective-permute-start) | collective-permute-done | bytes 262176 | tf_op jit(solution)/shard_map/while/body/eval_jaxpr/ppermute | solution.py:16
  57.6 1.9 collective-permute-start
  59.5 7.8 %collective-permute-done = f32[512,128]{1,0:T(8,128)S(1)} collective-permute-done((f32[512,128]{1,0:T(8,128)}, f32[512,128]{1,0:T(8,128)S(1)}, u32[]{:S(2)}, u32[]{:S(2)}) %collective-permute-start) | collective-permute-done | bytes 262176 | tf_op jit(solution)/shard_map/while/body/eval_jaxpr/ppermute | solution.py:16
  69.0 1.9 collective-permute-start
  70.9 7.8 %collective-permute-done = f32[512,128]{1,0:T(8,128)S(1)} collective-permute-done((f32[512,128]{1,0:T(8,128)}, f32[512,128]{1,0:T(8,128)S(1)}, u32[]{:S(2)}, u32[]{:S(2)}) %collective-permute-start) | collective-permute-done | bytes 262176 | tf_op jit(solution)/shard_map/while/body/eval_jaxpr/ppermute | solution.py:16
  80.4 1.9 collective-permute-start
  82.3 7.8 %collective-permute-done = f32[512,128]{1,0:T(8,128)S(1)} collective-permute-done((f32[512,128]{1,0:T(8,128)}, f32[512,128]{1,0:T(8,128)S(1)}, u32[]{:S(2)}, u32[]{:S(2)}) %collective-permute-start) | collective-permute-done | bytes 262176 | tf_op jit(solution)/shard_map/while/body/eval_jaxpr/ppermute | solution.py:16
  91.8 1.9 collective-permute-start
  93.7 7.8 %collective-permute-done = f32[512,128]{1,0:T(8,128)S(1)} collective-permute-done((f32[512,128]{1,0:T(8,128)}, f32[512,128]{1,0:T(8,128)S(1)}, u32[]{:S(2)}, u32[]{:S(2)}) %collective-permute-start) | collective-permute-done | bytes 262176 | tf_op jit(solution)/shard_map/while/body/eval_jaxpr/ppermute | solution.py:16
  103.2 1.9 collective-permute-start
  105.1 8.1 %collective-permute-done = f32[512,128]{1,0:T(8,128)S(1)} collective-permute-done((f32[512,128]{1,0:T(8,128)}, f32[512,128]{1,0:T(8,128)S(1)}, u32[]{:S(2)}, u32[]{:S(2)}) %collective-permute-start) | collective-permute-done | bytes 262176 | tf_op jit(solution)/shard_map/while/body/eval_jaxpr/ppermute | solution.py:16
  116.9 9.3 %collective-permute-done = f32[512,128]{1,0:T(8,128)S(1)} collective-permute-done((f32[512,128]{1,0:T(8,128)}, f32[512,128]{1,0:T(8,128)S(1)}, u32[]{:S(2)}, u32[]{:S(2)}) %collective-permute-start) | collective-permute-done | bytes 262176 | tf_op jit(solution)/shard_map/while/body/eval_jaxpr/ppermute | solution.py:16
  129.8 10.4 %collective-permute-done = f32[512,128]{1,0:T(8,128)S(1)} collective-permute-done((f32[512,128]{1,0:T(8,128)}, f32[512,128]{1,0:T(8,128)S(1)}, u32[]{:S(2)}, u32[]{:S(2)}) %collective-permute-start) | collective-permute-done | bytes 262176 | tf_op jit(solution)/shard_map/while/body/eval_jaxpr/ppermute | solution.py:16
  143.9 9.7 %collective-permute-done = f32[512,128]{1,0:T(8,128)S(1)} collective-permute-done((f32[512,128]{1,0:T(8,128)}, f32[512,128]{1,0:T(8,128)S(1)}, u32[]{:S(2)}, u32[]{:S(2)}) %collective-permute-start) | collective-permute-done | bytes 262176 | tf_op jit(solution)/shard_map/while/body/eval_jaxpr/ppermute | solution.py:16
  157.3 8.9 %collective-permute-done = f32[512,128]{1,0:T(8,128)S(1)} collective-permute-done((f32[512,128]{1,0:T(8,128)}, f32[512,128]{1,0:T(8,128)S(1)}, u32[]{:S(2)}, u32[]{:S(2)}) %collective-permute-start) | collective-permute-done | bytes 262176 | tf_op jit(solution)/shard_map/while/body/eval_jaxpr/ppermute | solution.py:16
  169.8 8.0 %collective-permute-done = f32[512,128]{1,0:T(8,128)S(1)} collective-permute-done((f32[512,128]{1,0:T(8,128)}, f32[512,128]{1,0:T(8,128)S(1)}, u32[]{:S(2)}, u32[]{:S(2)}) %collective-permute-start) | collective-permute-done | bytes 262176 | tf_op jit(solution)/shard_map/while/body/eval_jaxpr/ppermute | solution.py:16
  181.4 7.8 %collective-permute-done = f32[512,128]{1,0:T(8,128)S(1)} collective-permute-done((f32[512,128]{1,0:T(8,128)}, f32[512,128]{1,0:T(8,128)S(1)}, u32[]{:S(2)}, u32[]{:S(2)}) %collective-permute-start) | collective-permute-done | bytes 262176 | tf_op jit(solution)/shard_map/while/body/eval_jaxpr/ppermute | solution.py:16
  192.8 7.8 %collective-permute-done = f32[512,128]{1,0:T(8,128)S(1)} collective-permute-done((f32[512,128]{1,0:T(8,128)}, f32[512,128]{1,0:T(8,128)S(1)}, u32[]{:S(2)}, u32[]{:S(2)}) %collective-permute-start) | collective-permute-done | bytes 262176 | tf_op jit(solution)/shard_map/while/body/eval_jaxpr/ppermute | solution.py:16
  204.2 7.8 %collective-permute-done = f32[512,128]{1,0:T(8,128)S(1)} collective-permute-done((f32[512,128]{1,0:T(8,128)}, f32[512,128]{1,0:T(8,128)S(1)}, u32[]{:S(2)}, u32[]{:S(2)}) %collective-permute-start) | collective-permute-done | bytes 262176 | tf_op jit(solution)/shard_map/while/body/eval_jaxpr/ppermute | solution.py:16
  214.6 2.4 %collective-permute-start.1 = (bf16[128,128]{1,0:T(8,128)(2,1)S(1)}, bf16[128,128]{1,0:T(8,128)(2,1)S(1)}, u32[]{:S(2)}, u32[]{:S(2)}) collective-permute-start(bf16[128,128]{1,0:T(8,128)(2,1)S(1)} %fusion.3), channel_id=1, source_target_pairs={{0,2},{1,3},{2,4},{3,5},{4,6},{5,7},{6,8},{7,9},{8,10},{9,11},{10,... | collective-permute-start | bytes 98312 | tf_op jit(solution)/shard_map/ppermute | solution.py:10
  217.1 6.7 %collective-permute-start.4 = (bf16[128,128]{1,0:T(8,128)(2,1)S(1)}, bf16[128,128]{1,0:T(8,128)(2,1)S(1)}, u32[]{:S(2)}, u32[]{:S(2)}) collective-permute-start(bf16[128,128]{1,0:T(8,128)(2,1)S(1)} %fusion.3), channel_id=1, source_target_pairs={{0,30},{1,31},{2,0},{3,1},{4,2},{5,3},{6,4},{7,5},{8,6},{9,7},{10,... | collective-permute-start | bytes 98312 | tf_op jit(solution)/shard_map/ppermute | solution.py:10
  223.8 1.9 collective-permute-start.3
  225.8 2.4 %collective-permute-start.2 = (bf16[128,128]{1,0:T(8,128)(2,1)S(1)}, bf16[128,128]{1,0:T(8,128)(2,1)S(1)}, u32[]{:S(2)}, u32[]{:S(2)}) collective-permute-start(bf16[128,128]{1,0:T(8,128)(2,1)S(1)} %fusion.3), channel_id=1, source_target_pairs={{0,1},{1,2},{2,3},{3,4},{4,5},{5,6},{6,7},{7,8},{8,9},{9,10},{10,1... | collective-permute-start | bytes 98312 | tf_op jit(solution)/shard_map/ppermute | solution.py:10
  228.2 6.1 %collective-permute-done.2 = bf16[128,128]{1,0:T(8,128)(2,1)S(1)} collective-permute-done((bf16[128,128]{1,0:T(8,128)(2,1)S(1)}, bf16[128,128]{1,0:T(8,128)(2,1)S(1)}, u32[]{:S(2)}, u32[]{:S(2)}) %collective-permute-start.2) | collective-permute-done | bytes 32800 | tf_op jit(solution)/shard_map/ppermute | solution.py:10
  (76 shorter events, 51.6 us)
Async XLA Ops:
  0.6 234.4 %copy-start = (bf16[1,1,1536,512]{3,2,1,0:T(8,128)(2,1)S(1)}, bf16[1,1,1536,512]{3,2,1,0:T(8,128)(2,1)}, u32[]{:S(2)}) copy-start(bf16[1,1,1536,512]{3,2,1,0:T(8,128)(2,1)} %param.22) | copy-start | bytes 4718596
  0.6 18.1 %copy-start.1 = (f32[1,512,512]{2,1,0:T(8,128)S(1)}, f32[1,512,512]{2,1,0:T(8,128)}, u32[]{:S(2)}) copy-start(f32[1,512,512]{2,1,0:T(8,128)} %param.15) | copy-start | bytes 3145732
  2.5 16.2 %all-to-all-start = ((f32[32,16,128]{2,1,0:T(8,128)}), f32[32,16,128]{2,1,0:T(8,128)S(1)}, u32[]{:S(2)}, u32[]{:S(2)}) async-start(f32[32,16,128]{2,1,0:T(8,128)} %stack.14), calls=%async_computation | async-start | bytes 524288 | tf_op jit(solution)/shard_map/all_to_all | solution.py:50
  18.8 195.7 %copy-start.5 = (bf16[1,1,128,128]{3,2,1,0:T(8,128)(2,1)S(1)}, bf16[1,1,128,128]{3,2,1,0:T(8,128)(2,1)}, u32[]{:S(2)}) copy-start(bf16[1,1,128,128]{3,2,1,0:T(8,128)(2,1)} %param.18) | copy-start | bytes 98308
  18.8 195.7 %copy-start.6 = (bf16[1,1,128,128]{3,2,1,0:T(8,128)(2,1)S(1)}, bf16[1,1,128,128]{3,2,1,0:T(8,128)(2,1)}, u32[]{:S(2)}) copy-start(bf16[1,1,128,128]{3,2,1,0:T(8,128)(2,1)} %param.17) | copy-start | bytes 98308
  19.5 11.8 %collective-permute-start = (f32[512,128]{1,0:T(8,128)}, f32[512,128]{1,0:T(8,128)S(1)}, u32[]{:S(2)}, u32[]{:S(2)}) collective-permute-start(f32[512,128]{1,0:T(8,128)} %broadcast_select_fusion.3), channel_id=1, source_target_pairs={{0,32},{32,64},{64,96},{96,128},{128,160},{160,192},{192,224},{224... | collective-permute-start | bytes 786440 | tf_op jit(solution)/shard_map/while/body/eval_jaxpr/ppermute | solution.py:16
  33.1 11.0 %collective-permute-start = (f32[512,128]{1,0:T(8,128)}, f32[512,128]{1,0:T(8,128)S(1)}, u32[]{:S(2)}, u32[]{:S(2)}) collective-permute-start(f32[512,128]{1,0:T(8,128)} %broadcast_select_fusion.3), channel_id=1, source_target_pairs={{0,32},{32,64},{64,96},{96,128},{128,160},{160,192},{192,224},{224... | collective-permute-start | bytes 786440 | tf_op jit(solution)/shard_map/while/body/eval_jaxpr/ppermute | solution.py:16
  45.8 10.1 %collective-permute-start = (f32[512,128]{1,0:T(8,128)}, f32[512,128]{1,0:T(8,128)S(1)}, u32[]{:S(2)}, u32[]{:S(2)}) collective-permute-start(f32[512,128]{1,0:T(8,128)} %broadcast_select_fusion.3), channel_id=1, source_target_pairs={{0,32},{32,64},{64,96},{96,128},{128,160},{160,192},{192,224},{224... | collective-permute-start | bytes 786440 | tf_op jit(solution)/shard_map/while/body/eval_jaxpr/ppermute | solution.py:16
  57.6 9.7 %collective-permute-start = (f32[512,128]{1,0:T(8,128)}, f32[512,128]{1,0:T(8,128)S(1)}, u32[]{:S(2)}, u32[]{:S(2)}) collective-permute-start(f32[512,128]{1,0:T(8,128)} %broadcast_select_fusion.3), channel_id=1, source_target_pairs={{0,32},{32,64},{64,96},{96,128},{128,160},{160,192},{192,224},{224... | collective-permute-start | bytes 786440 | tf_op jit(solution)/shard_map/while/body/eval_jaxpr/ppermute | solution.py:16
  69.0 9.7 %collective-permute-start = (f32[512,128]{1,0:T(8,128)}, f32[512,128]{1,0:T(8,128)S(1)}, u32[]{:S(2)}, u32[]{:S(2)}) collective-permute-start(f32[512,128]{1,0:T(8,128)} %broadcast_select_fusion.3), channel_id=1, source_target_pairs={{0,32},{32,64},{64,96},{96,128},{128,160},{160,192},{192,224},{224... | collective-permute-start | bytes 786440 | tf_op jit(solution)/shard_map/while/body/eval_jaxpr/ppermute | solution.py:16
  80.4 9.7 %collective-permute-start = (f32[512,128]{1,0:T(8,128)}, f32[512,128]{1,0:T(8,128)S(1)}, u32[]{:S(2)}, u32[]{:S(2)}) collective-permute-start(f32[512,128]{1,0:T(8,128)} %broadcast_select_fusion.3), channel_id=1, source_target_pairs={{0,32},{32,64},{64,96},{96,128},{128,160},{160,192},{192,224},{224... | collective-permute-start | bytes 786440 | tf_op jit(solution)/shard_map/while/body/eval_jaxpr/ppermute | solution.py:16
  91.8 9.7 %collective-permute-start = (f32[512,128]{1,0:T(8,128)}, f32[512,128]{1,0:T(8,128)S(1)}, u32[]{:S(2)}, u32[]{:S(2)}) collective-permute-start(f32[512,128]{1,0:T(8,128)} %broadcast_select_fusion.3), channel_id=1, source_target_pairs={{0,32},{32,64},{64,96},{96,128},{128,160},{160,192},{192,224},{224... | collective-permute-start | bytes 786440 | tf_op jit(solution)/shard_map/while/body/eval_jaxpr/ppermute | solution.py:16
  103.2 10.0 %collective-permute-start = (f32[512,128]{1,0:T(8,128)}, f32[512,128]{1,0:T(8,128)S(1)}, u32[]{:S(2)}, u32[]{:S(2)}) collective-permute-start(f32[512,128]{1,0:T(8,128)} %broadcast_select_fusion.3), channel_id=1, source_target_pairs={{0,32},{32,64},{64,96},{96,128},{128,160},{160,192},{192,224},{224... | collective-permute-start | bytes 786440 | tf_op jit(solution)/shard_map/while/body/eval_jaxpr/ppermute | solution.py:16
  115.0 11.2 %collective-permute-start = (f32[512,128]{1,0:T(8,128)}, f32[512,128]{1,0:T(8,128)S(1)}, u32[]{:S(2)}, u32[]{:S(2)}) collective-permute-start(f32[512,128]{1,0:T(8,128)} %broadcast_select_fusion.3), channel_id=1, source_target_pairs={{0,32},{32,64},{64,96},{96,128},{128,160},{160,192},{192,224},{224... | collective-permute-start | bytes 786440 | tf_op jit(solution)/shard_map/while/body/eval_jaxpr/ppermute | solution.py:16
  127.9 12.3 %collective-permute-start = (f32[512,128]{1,0:T(8,128)}, f32[512,128]{1,0:T(8,128)S(1)}, u32[]{:S(2)}, u32[]{:S(2)}) collective-permute-start(f32[512,128]{1,0:T(8,128)} %broadcast_select_fusion.3), channel_id=1, source_target_pairs={{0,32},{32,64},{64,96},{96,128},{128,160},{160,192},{192,224},{224... | collective-permute-start | bytes 786440 | tf_op jit(solution)/shard_map/while/body/eval_jaxpr/ppermute | solution.py:16
  142.0 11.6 %collective-permute-start = (f32[512,128]{1,0:T(8,128)}, f32[512,128]{1,0:T(8,128)S(1)}, u32[]{:S(2)}, u32[]{:S(2)}) collective-permute-start(f32[512,128]{1,0:T(8,128)} %broadcast_select_fusion.3), channel_id=1, source_target_pairs={{0,32},{32,64},{64,96},{96,128},{128,160},{160,192},{192,224},{224... | collective-permute-start | bytes 786440 | tf_op jit(solution)/shard_map/while/body/eval_jaxpr/ppermute | solution.py:16
  155.3 10.8 %collective-permute-start = (f32[512,128]{1,0:T(8,128)}, f32[512,128]{1,0:T(8,128)S(1)}, u32[]{:S(2)}, u32[]{:S(2)}) collective-permute-start(f32[512,128]{1,0:T(8,128)} %broadcast_select_fusion.3), channel_id=1, source_target_pairs={{0,32},{32,64},{64,96},{96,128},{128,160},{160,192},{192,224},{224... | collective-permute-start | bytes 786440 | tf_op jit(solution)/shard_map/while/body/eval_jaxpr/ppermute | solution.py:16
  167.9 9.9 %collective-permute-start = (f32[512,128]{1,0:T(8,128)}, f32[512,128]{1,0:T(8,128)S(1)}, u32[]{:S(2)}, u32[]{:S(2)}) collective-permute-start(f32[512,128]{1,0:T(8,128)} %broadcast_select_fusion.3), channel_id=1, source_target_pairs={{0,32},{32,64},{64,96},{96,128},{128,160},{160,192},{192,224},{224... | collective-permute-start | bytes 786440 | tf_op jit(solution)/shard_map/while/body/eval_jaxpr/ppermute | solution.py:16
  179.5 9.7 %collective-permute-start = (f32[512,128]{1,0:T(8,128)}, f32[512,128]{1,0:T(8,128)S(1)}, u32[]{:S(2)}, u32[]{:S(2)}) collective-permute-start(f32[512,128]{1,0:T(8,128)} %broadcast_select_fusion.3), channel_id=1, source_target_pairs={{0,32},{32,64},{64,96},{96,128},{128,160},{160,192},{192,224},{224... | collective-permute-start | bytes 786440 | tf_op jit(solution)/shard_map/while/body/eval_jaxpr/ppermute | solution.py:16
  190.9 9.7 %collective-permute-start = (f32[512,128]{1,0:T(8,128)}, f32[512,128]{1,0:T(8,128)S(1)}, u32[]{:S(2)}, u32[]{:S(2)}) collective-permute-start(f32[512,128]{1,0:T(8,128)} %broadcast_select_fusion.3), channel_id=1, source_target_pairs={{0,32},{32,64},{64,96},{96,128},{128,160},{160,192},{192,224},{224... | collective-permute-start | bytes 786440 | tf_op jit(solution)/shard_map/while/body/eval_jaxpr/ppermute | solution.py:16
  202.3 9.7 %collective-permute-start = (f32[512,128]{1,0:T(8,128)}, f32[512,128]{1,0:T(8,128)S(1)}, u32[]{:S(2)}, u32[]{:S(2)}) collective-permute-start(f32[512,128]{1,0:T(8,128)} %broadcast_select_fusion.3), channel_id=1, source_target_pairs={{0,32},{32,64},{64,96},{96,128},{128,160},{160,192},{192,224},{224... | collective-permute-start | bytes 786440 | tf_op jit(solution)/shard_map/while/body/eval_jaxpr/ppermute | solution.py:16
  213.0 22.7 %copy-start.2 = (f32[512,128]{1,0:T(8,128)}, f32[512,128]{1,0:T(8,128)S(1)}, u32[]{:S(2)}) copy-start(f32[512,128]{1,0:T(8,128)S(1)} %get-tuple-element.25) | copy-start | bytes 786436
  213.0 22.1 %copy-start.3 = (f32[128,1536]{1,0:T(8,128)S(1)}, f32[128,1536]{1,0:T(8,128)}, u32[]{:S(2)}) copy-start(f32[128,1536]{1,0:T(8,128)} %fusion.4) | copy-start | bytes 2359300
  214.6 21.1 %copy-start.4 = (bf16[128,128]{1,0:T(8,128)(2,1)}, bf16[128,128]{1,0:T(8,128)(2,1)S(1)}, u32[]{:S(2)}) copy-start(bf16[128,128]{1,0:T(8,128)(2,1)S(1)} %fusion.3) | copy-start | bytes 98308
  214.6 13.5 %collective-permute-start.1 = (bf16[128,128]{1,0:T(8,128)(2,1)S(1)}, bf16[128,128]{1,0:T(8,128)(2,1)S(1)}, u32[]{:S(2)}, u32[]{:S(2)}) collective-permute-start(bf16[128,128]{1,0:T(8,128)(2,1)S(1)} %fusion.3), channel_id=1, source_target_pairs={{0,2},{1,3},{2,4},{3,5},{4,6},{5,7},{6,8},{7,9},{8,10},{9,11},{10,... | collective-permute-start | bytes 98312 | tf_op jit(solution)/shard_map/ppermute | solution.py:10
  217.1 17.3 %collective-permute-start.4 = (bf16[128,128]{1,0:T(8,128)(2,1)S(1)}, bf16[128,128]{1,0:T(8,128)(2,1)S(1)}, u32[]{:S(2)}, u32[]{:S(2)}) collective-permute-start(bf16[128,128]{1,0:T(8,128)(2,1)S(1)} %fusion.3), channel_id=1, source_target_pairs={{0,30},{1,31},{2,0},{3,1},{4,2},{5,3},{6,4},{7,5},{8,6},{9,7},{10,... | collective-permute-start | bytes 98312 | tf_op jit(solution)/shard_map/ppermute | solution.py:10
  223.8 10.5 %collective-permute-start.3 = (bf16[128,128]{1,0:T(8,128)(2,1)S(1)}, bf16[128,128]{1,0:T(8,128)(2,1)S(1)}, u32[]{:S(2)}, u32[]{:S(2)}) collective-permute-start(bf16[128,128]{1,0:T(8,128)(2,1)S(1)} %fusion.3), channel_id=1, source_target_pairs={{0,31},{1,0},{2,1},{3,2},{4,3},{5,4},{6,5},{7,6},{8,7},{9,8},{10,9... | collective-permute-start | bytes 98312 | tf_op jit(solution)/shard_map/ppermute | solution.py:10
  225.8 8.6 %collective-permute-start.2 = (bf16[128,128]{1,0:T(8,128)(2,1)S(1)}, bf16[128,128]{1,0:T(8,128)(2,1)S(1)}, u32[]{:S(2)}, u32[]{:S(2)}) collective-permute-start(bf16[128,128]{1,0:T(8,128)(2,1)S(1)} %fusion.3), channel_id=1, source_target_pairs={{0,1},{1,2},{2,3},{3,4},{4,5},{5,6},{6,7},{7,8},{8,9},{9,10},{10,1... | collective-permute-start | bytes 98312 | tf_op jit(solution)/shard_map/ppermute | solution.py:10
